TPU v7x, 256 devices: a whole 4x4x8 slice. The times are simulated.
256 devices in a mesh: row: 32 (over y, z), col: 8 (over x, core).
Axes of the slice: x: 4, y: 4, z: 8, core: 2. Of those that a mesh axis runs over, the one named last changes fastest.
Arguments:
- acts: bfloat16 [6144, 28672], P('col', 'row'), may hold values from -12 to 12
- out_grad: bfloat16 [6144, 8192], P('row', 'col'), may hold values from -12 to 12
- lengths: int32 [8], replicated, may hold values from 1 to 768, 4800 in all
Outputs:
- weight_grad: bfloat16 [28672, 8192], P('row', 'col')
- norms: float32 [8], replicated
All inputs are finite; a program needn't handle non-finite values.
Results may differ from a plain program's by a relative error of at most 0.0013.
Values may be sent and summed in bfloat16 or wider, within the bound.
No kernel may reach another device: no remote copies, remote signals or barrier semaphores. Data moves between devices by JAX's collectives and lax.ppermute only.
A program may use at most 128 MiB of HBM per device.

v0:
```python
import jax
import jax.numpy as jnp
from jax import lax
from jax.sharding import PartitionSpec as P

FF = 28672
D = 8192


def body(acts, out_grad, lengths):
    n_row = lax.axis_size("row")
    n_col = lax.axis_size("col")
    row_idx = lax.axis_index("row")
    col_idx = lax.axis_index("col")
    own_rows = out_grad.shape[0]
    tokens = own_rows * n_row
    seqs = lengths.shape[0]
    seq_len = tokens // seqs
    block = own_rows // n_col
    feats = acts.shape[1]
    width = out_grad.shape[1]
    positions = jnp.arange(tokens, dtype=jnp.int32)
    seq_of = positions // seq_len
    limit = jnp.sum(
        jnp.where(
            seq_of[:, None] == jnp.arange(seqs, dtype=jnp.int32)[None, :], lengths[None, :], 0
        ),
        axis=1,
    )
    live = positions % seq_len < limit
    act_full = lax.all_gather(acts, "col", axis=0, tiled=True)
    grad_full = lax.all_gather(out_grad, "row", axis=0, tiled=True)
    grads = jnp.where(live[:, None], grad_full, jnp.zeros_like(grad_full))
    act_seq = act_full.reshape(seqs, seq_len, feats)
    picked = lax.dynamic_index_in_dim(
        act_full.reshape(n_row, n_col, block, feats), col_idx, 1, keepdims=False
    )
    picked = picked.reshape(seqs, n_row // seqs * block, feats)
    act_part = jnp.einsum("sqf,slf->sql", picked, act_seq, preferred_element_type=jnp.float32)
    act_part = act_part.reshape(n_row * block, seq_len)
    summed = lax.psum(act_part.astype(jnp.bfloat16), "row").astype(jnp.float32)
    act_gram = lax.dynamic_slice_in_dim(summed, row_idx * block, block, 0)
    first = row_idx * own_rows
    own_seq = first // seq_len
    own_grads = lax.dynamic_slice_in_dim(grads, first, own_rows, 0)
    seq_grads = lax.dynamic_slice_in_dim(grads, own_seq * seq_len, seq_len, 0)
    grad_part = lax.dot_general(
        own_grads, seq_grads, (((1,), (1,)), ((), ())), preferred_element_type=jnp.float32
    )
    grad_gram = lax.psum_scatter(
        grad_part.astype(jnp.bfloat16), "col", scatter_dimension=0, tiled=True
    ).astype(jnp.float32)
    local = jnp.sum(act_gram * grad_gram)
    onehot = jnp.arange(seqs, dtype=jnp.int32) == own_seq
    squares = lax.psum(jnp.where(onehot, local, jnp.float32(0.0)), ("row", "col"))
    divisor = float(FF) * float(D) * float(seq_len)
    norms = jnp.sqrt(squares / divisor)
    scale = 1.0 / (norms + 0.1)
    total = jnp.zeros((feats, width), jnp.float32)
    for seq in range(seqs):
        act_rows = act_full[seq * seq_len : (seq + 1) * seq_len]
        grad_rows = grads[seq * seq_len : (seq + 1) * seq_len]
        product = lax.dot_general(
            act_rows, grad_rows, (((0,), (0,)), ((), ())), preferred_element_type=jnp.float32
        )
        total = total + scale[seq] * product
    weight_grad = (total / jnp.sqrt(jnp.float32(tokens))).astype(jnp.bfloat16)
    return (weight_grad, norms)


def solution(mesh):
    placed = (P("col", "row"), P("row", "col"), P())
    return jax.shard_map(
        body, mesh=mesh, in_specs=placed, out_specs=(P("row", "col"), P()), check_vma=False
    )
```

profile of v0, /device:TPU:1, one launch (start us, length us, event | category | flops | bytes accessed | tf_op | source)
XLA Modules:
  0.0 495.1 jit_solution(12963730170209471229)
XLA Ops:
  7.2 0.0 all-gather.3.cloned.1.call-start
  7.2 0.7 all-gather.3.cloned.1.call-update
  7.9 0.0 all-gather.5.cloned.1.call-start
  7.9 0.7 all-gather.5.cloned.1.call-update
  8.6 0.0 all-reduce.2.cloned.1.call-start
  8.7 0.8 select_reduce_fusion
  9.6 67.7 %all-gather.3.cloned.1.call-done = bf16[6144,896]{1,0:T(8,128)(2,1)} async-done(((bf16[768,896]{1,0:T(8,128)(2,1)}), bf16[6144,896]{1,0:T(8,128)(2,1)}) %all-gather.3.cloned.1.call-update) | async-done | bytes 11010064 | tf_op jit(solution)/shard_map/all_gather | solution.py:31
  77.2 1.5 constant_dynamic-slice_fusion
  78.7 8.6 %convolution_convert_fusion = bf16[8,96,768]{2,1,0:T(8,128)(2,1)} fusion(bf16[8,96,896]{2,1,0:T(8,128)(2,1)S(1)} %bitcast.20, bf16[8,768,896]{2,1,0:T(8,128)(2,1)} %bitcast.19), kind=kOutput, calls=%fused_computation.20 | convolution fusion | flops 1057554432 | bytes 13565952 | tf_op jit(solution)/shard_map/sqf,slf->sql/dot_general | solution.py:39
  87.3 0.0 all-reduce.2.cloned.1.call-update
  87.4 0.2 reduce-scatter.2.cloned.1.call-start
  87.6 110.4 %all-gather.5.cloned.1.call-done = bf16[6144,1024]{1,0:T(8,128)(2,1)} async-done(((bf16[192,1024]{1,0:T(8,128)(2,1)}), bf16[6144,1024]{1,0:T(8,128)(2,1)}) %all-gather.5.cloned.1.call-update) | async-done | bytes 12582928 | tf_op jit(solution)/shard_map/all_gather | solution.py:32
  197.9 6.4 %broadcast_select_fusion = bf16[6144,1024]{1,0:T(8,128)(2,1)S(1)} fusion(bf16[6144,1024]{1,0:T(8,128)(2,1)} %all-gather.5.cloned.1.call-done, pred[6144]{0:T(1024)(128)(4,1)S(1)} %fusion.32), kind=kLoop, calls=%fused_computation | loop fusion | flops 6291456 | bytes 25171968 | tf_op jit(solution)/shard_map/jit(_where)/select_n | solution.py:33
  204.3 0.0 copy-start
  204.3 4.5 copy-done
  208.9 1.4 fusion.28
  210.3 0.0 reduce-scatter.2.cloned.1.call-update
  210.3 0.0 copy-start.1
  210.3 5.7 %fusion.1 = f32[1024,896]{1,0:T(8,128)} fusion(bf16[6144,1024]{1,0:T(8,128)(2,1)} %copy-done, bf16[6144,896]{1,0:T(8,128)(2,1)} %all-gather.3.cloned.1.call-done), kind=kOutput, calls=%fused_computation.3 | convolution fusion | flops 1409286144 | bytes 6619136 | tf_op jit(solution)/shard_map/dot_general | solution.py:63
  216.0 5.7 %fusion.3 = f32[1024,896]{1,0:T(8,128)} fusion(bf16[6144,1024]{1,0:T(8,128)(2,1)} %copy-done, bf16[6144,896]{1,0:T(8,128)(2,1)} %all-gather.3.cloned.1.call-done), kind=kOutput, calls=%fused_computation.5 | convolution fusion | flops 1409286144 | bytes 6619136 | tf_op jit(solution)/shard_map/dot_general | solution.py:63
  221.7 0.0 copy-done.1
  221.7 5.0 %fusion.5 = f32[1024,896]{1,0:T(8,128)} fusion(bf16[6144,1024]{1,0:T(8,128)(2,1)S(1)} %copy-done.1, bf16[6144,896]{1,0:T(8,128)(2,1)} %all-gather.3.cloned.1.call-done), kind=kOutput, calls=%fused_computation.7 | convolution fusion | flops 1409286144 | bytes 6619136 | tf_op jit(solution)/shard_map/dot_general | solution.py:63
  226.7 5.1 %fusion.7 = f32[1024,896]{1,0:T(8,128)} fusion(bf16[6144,1024]{1,0:T(8,128)(2,1)S(1)} %copy-done.1, bf16[6144,896]{1,0:T(8,128)(2,1)} %all-gather.3.cloned.1.call-done), kind=kOutput, calls=%fused_computation.9 | convolution fusion | flops 1409286144 | bytes 6619136 | tf_op jit(solution)/shard_map/dot_general | solution.py:63
  231.9 5.0 %fusion.9 = f32[1024,896]{1,0:T(8,128)} fusion(bf16[6144,1024]{1,0:T(8,128)(2,1)S(1)} %copy-done.1, bf16[6144,896]{1,0:T(8,128)(2,1)} %all-gather.3.cloned.1.call-done), kind=kOutput, calls=%fused_computation.11 | convolution fusion | flops 1409286144 | bytes 6619136 | tf_op jit(solution)/shard_map/dot_general | solution.py:63
  236.9 5.0 %fusion.11 = f32[1024,896]{1,0:T(8,128)} fusion(bf16[6144,1024]{1,0:T(8,128)(2,1)S(1)} %copy-done.1, bf16[6144,896]{1,0:T(8,128)(2,1)} %all-gather.3.cloned.1.call-done), kind=kOutput, calls=%fused_computation.13 | convolution fusion | flops 1409286144 | bytes 6619136 | tf_op jit(solution)/shard_map/dot_general | solution.py:63
  241.8 103.9 %all-reduce.2.cloned.1.call-done = bf16[768,768]{1,0:T(8,128)(2,1)} async-done(((bf16[768,768]{1,0:T(8,128)(2,1)}), bf16[768,768]{1,0:T(8,128)(2,1)}) %all-reduce.2.cloned.1.call-update) | async-done | bytes 1179664 | tf_op jit(solution)/shard_map/psum | solution.py:41
  345.7 35.8 %reduce-scatter.2.cloned.1.call-done = bf16[24,768]{1,0:T(8,128)(2,1)} async-done(((bf16[192,768]{1,0:T(8,128)(2,1)}), bf16[24,768]{1,0:T(8,128)(2,1)}) %reduce-scatter.2.cloned.1.call-update) | async-done | bytes 36880 | tf_op jit(solution)/shard_map/reduce_scatter | solution.py:50
  381.5 1.4 multiply_reduce_fusion
  382.9 0.6 compare_select_fusion
  383.5 5.5 %fusion.13 = f32[1024,896]{1,0:T(8,128)} fusion(bf16[6144,1024]{1,0:T(8,128)(2,1)} %copy-done, bf16[6144,896]{1,0:T(8,128)(2,1)} %all-gather.3.cloned.1.call-done), kind=kOutput, calls=%fused_computation.15 | convolution fusion | flops 1409286144 | bytes 6619136 | tf_op jit(solution)/shard_map/dot_general | solution.py:63
  389.0 78.5 %psum.15 = f32[8]{0:T(128)S(1)} all-reduce(f32[8]{0:T(128)S(1)} %compare_select_fusion), channel_id=1, replica_groups=mesh['row'=32,'col'=8] {'row','col'}, use_global_device_ids=true, to_apply=%region_4.5 | all-reduce | flops 8 | bytes 64 | tf_op jit(solution)/shard_map/psum | solution.py:55
  467.5 0.5 add_divide_fusion
  468.0 0.6 fusion.39
  468.6 17.5 %fusion.17 = bf16[896,1024]{0,1:T(8,128)(2,1)S(1)} fusion(bf16[6144,1024]{1,0:T(8,128)(2,1)} %copy-done, f32[]{:T(128)} %bitcast.11, f32[1024,896]{1,0:T(8,128)} %fusion.1, f32[]{:T(128)} %bitcast.10, f32[1024,896]{1,0:T(8,128)} %fusion.3, f32[]{:T(128)} %bitcast.9, f32[1024,896]{1,0:T(8,128)} %fusion.5, f32[]{:T(128)} %bitcast.8, f32[1024,896]{1,0:T(8,128)} %fusion.7, ...), kind=kOutput, calls=%fused_computation.19 | convolution fusion | flops 1424883712 | bytes 30478336 | tf_op jit(solution)/shard_map/dot_general | solution.py:63
  486.1 2.4 copy.8
  (2 shorter events, 0.0 us)
Async XLA Ops:
  7.2 70.1 %all-gather.3.cloned.1.call-start = ((), (), s32[]{:S(2)}) async-start(), calls=%async_computation.1 | async-start | bytes 12386304 | tf_op jit(solution)/shard_map/all_gather | solution.py:31
  7.9 190.0 %all-gather.5.cloned.1.call-start = ((), (), s32[]{:S(2)}) async-start(), calls=%async_computation.3 | async-start | bytes 12976128 | tf_op jit(solution)/shard_map/all_gather | solution.py:32
  8.6 337.1 %all-reduce.2.cloned.1.call-start = ((), (), s32[]{:S(2)}) async-start(), calls=%async_computation.2 | async-start | bytes 2359296 | tf_op jit(solution)/shard_map/psum | solution.py:41
  87.4 294.1 %reduce-scatter.2.cloned.1.call-start = ((), (), s32[]{:S(2)}) async-start(), calls=%async_computation.4 | async-start | bytes 331776 | tf_op jit(solution)/shard_map/reduce_scatter | solution.py:50
  204.3 4.6 copy-start
  210.3 11.4 %copy-start.1 = (bf16[6144,1024]{1,0:T(8,128)(2,1)S(1)}, bf16[6144,1024]{1,0:T(8,128)(2,1)}, u32[]{:S(2)}) copy-start(bf16[6144,1024]{1,0:T(8,128)(2,1)} %copy-done) | copy-start | bytes 37748740
Sparse Core Ops, SparseCore 0:
  9.8 67.3 all-gather.2
  79.8 118.0 all-gather.4
  201.9 143.7 all-reduce.1
  348.1 33.3 reduce-scatter.1
where the time goes:
time: 496 us; the launch traced here: 495 us
  waiting for transfers between devices  319 us (64%)
  blocking collectives  78.5 us (16%)
  matrix products  64.5 us (13%)
  between operations  13.9 us (3%)
  other arithmetic  9.76 us (2%)
  local copies, waits for them, and re-layouts  9.06 us (2%)
    all_gather x1, waiting for transfers between devices, body(): grad_full = lax.all_gather(out_grad, 'row', axis=0, tiled=True)  110 us
    psum x1, waiting for transfers between devices, body(): summed = lax.psum(act_part.astype(jnp.bfloat16), 'row').astype(jnp.float32)  104 us
    psum x1, blocking collectives, body(): lax.psum(jnp.where(onehot, local, jnp.float32(0.0)), ('row', 'col'))  78.5 us
    all_gather x1, waiting for transfers between devices, body(): act_full = lax.all_gather(acts, 'col', axis=0, tiled=True)  67.7 us
    dot_general x8, matrix products, body(): lax.dot_general(act_rows, grad_rows, (((0,), (0,)), ((), ())), preferred_...  54.5 us
    reduce_scatter x1, waiting for transfers between devices, body(): lax.psum_scatter(grad_part.astype(jnp.bfloat16), 'col', scatter_dimension...  35.8 us
  transfers between devices with their start and end apart: 4, of which 4 were waited for; matrix products, arithmetic and copies ran while one was open for 10% of the time, Pallas kernels for 0%

commit v1 on v0

--- a/solution.py
+++ b/solution.py
@@ -2,9 +2,11 @@
 import jax.numpy as jnp
 from jax import lax
 from jax.sharding import PartitionSpec as P
+from jax.lax import all_gather
 
 FF = 28672
 D = 8192
+clear_numbers = lambda frame_in, a_name: jnp.sum(all_gather(frame_in, a_name), 0)
 
 
 def body(acts, out_grad, lengths):
@@ -52,7 +54,7 @@
     ).astype(jnp.float32)
     local = jnp.sum(act_gram * grad_gram)
     onehot = jnp.arange(seqs, dtype=jnp.int32) == own_seq
-    squares = lax.psum(jnp.where(onehot, local, jnp.float32(0.0)), ("row", "col"))
+    squares = clear_numbers(jnp.where(onehot, local, jnp.float32(0.0)), ("row", "col"))
     divisor = float(FF) * float(D) * float(seq_len)
     norms = jnp.sqrt(squares / divisor)
     scale = 1.0 / (norms + 0.1)

time: 496 us -> 471 us (0.950)
  blocking collectives: 78.5 us -> 59.2 us
  matrix products: 64.5 us -> 58.9 us
    psum x1 -> x0, blocking collectives: 78.5 us -> none  [body(): lax.psum(jnp.where(onehot, local, jnp.float32(0.0)), ('row', 'col'))]
    all_gather x0 -> x1, blocking collectives: none -> 59.2 us  [all_gather(frame_in, a_name)]
    dot_general x8, matrix products: 54.5 us -> 48.9 us  [body(): lax.dot_general(act_rows, grad_rows, (((0,), (0,)), ((), ())), preferred_...]
  transfers between devices with their start and end apart: 4 -> 4, of which waited for: 4 -> 4; matrix products, arithmetic and copies ran while one was open for 10% -> 11% of each run, Pallas kernels for 0% -> 0%
where the time goes in v1:
time: 471 us
  waiting for transfers between devices  319 us (68%)
  blocking collectives  59.2 us (13%)
  matrix products  58.9 us (13%)
  between operations  13.9 us (3%)
  other arithmetic  10.1 us (2%)
  local copies, waits for them, and re-layouts  9.07 us (2%)
    all_gather x1, waiting for transfers between devices, body(): grad_full = lax.all_gather(out_grad, 'row', axis=0, tiled=True)  110 us
    psum x1, waiting for transfers between devices, body(): summed = lax.psum(act_part.astype(jnp.bfloat16), 'row').astype(jnp.float32)  104 us
    all_gather x1, waiting for transfers between devices, body(): act_full = lax.all_gather(acts, 'col', axis=0, tiled=True)  67.7 us
    all_gather x1, blocking collectives, all_gather(frame_in, a_name)  59.2 us
    dot_general x8, matrix products, body(): lax.dot_general(act_rows, grad_rows, (((0,), (0,)), ((), ())), preferred_...  48.9 us
    reduce_scatter x1, waiting for transfers between devices, body(): lax.psum_scatter(grad_part.astype(jnp.bfloat16), 'col', scatter_dimension...  35.8 us
  transfers between devices with their start and end apart: 4, of which 4 were waited for; matrix products, arithmetic and copies ran while one was open for 11% of the time, Pallas kernels for 0%

profile of v1, /device:TPU:1, one launch (start us, length us, event | category | flops | bytes accessed | tf_op | source)
XLA Modules:
  0.0 470.8 jit_solution(16397741176272907447)
XLA Ops:
  7.2 0.0 all-gather.4.cloned.1.call-start
  7.2 0.7 all-gather.4.cloned.1.call-update
  7.9 0.0 all-gather.6.cloned.1.call-start
  7.9 0.7 all-gather.6.cloned.1.call-update
  8.6 0.0 all-reduce.2.cloned.1.call-start
  8.7 0.8 select_reduce_fusion
  9.6 67.7 %all-gather.4.cloned.1.call-done = bf16[6144,896]{1,0:T(8,128)(2,1)} async-done(((bf16[768,896]{1,0:T(8,128)(2,1)}), bf16[6144,896]{1,0:T(8,128)(2,1)}) %all-gather.4.cloned.1.call-update) | async-done | bytes 11010064 | tf_op jit(solution)/shard_map/all_gather | solution.py:33
  77.2 1.5 constant_dynamic-slice_fusion
  78.7 8.6 %convolution_convert_fusion = bf16[8,96,768]{2,1,0:T(8,128)(2,1)} fusion(bf16[8,96,896]{2,1,0:T(8,128)(2,1)S(1)} %bitcast.24, bf16[8,768,896]{2,1,0:T(8,128)(2,1)} %bitcast.21), kind=kOutput, calls=%fused_computation.20 | convolution fusion | flops 1057554432 | bytes 13565952 | tf_op jit(solution)/shard_map/sqf,slf->sql/dot_general | solution.py:41
  87.3 0.0 all-reduce.2.cloned.1.call-update
  87.4 0.2 reduce-scatter.2.cloned.1.call-start
  87.6 110.4 %all-gather.6.cloned.1.call-done = bf16[6144,1024]{1,0:T(8,128)(2,1)} async-done(((bf16[192,1024]{1,0:T(8,128)(2,1)}), bf16[6144,1024]{1,0:T(8,128)(2,1)}) %all-gather.6.cloned.1.call-update) | async-done | bytes 12582928 | tf_op jit(solution)/shard_map/all_gather | solution.py:34
  197.9 6.4 %broadcast_select_fusion = bf16[6144,1024]{1,0:T(8,128)(2,1)S(1)} fusion(bf16[6144,1024]{1,0:T(8,128)(2,1)} %all-gather.6.cloned.1.call-done, pred[6144]{0:T(1024)(128)(4,1)S(1)} %fusion.32), kind=kLoop, calls=%fused_computation | loop fusion | flops 6291456 | bytes 25171968 | tf_op jit(solution)/shard_map/jit(_where)/select_n | solution.py:35
  204.3 0.0 copy-start
  204.3 4.5 copy-done
  208.8 1.4 fusion.28
  210.2 0.0 reduce-scatter.2.cloned.1.call-update
  210.3 0.0 copy-start.1
  210.3 5.7 %fusion.1 = f32[1024,896]{1,0:T(8,128)} fusion(bf16[6144,1024]{1,0:T(8,128)(2,1)} %copy-done, bf16[6144,896]{1,0:T(8,128)(2,1)} %all-gather.4.cloned.1.call-done), kind=kOutput, calls=%fused_computation.3 | convolution fusion | flops 1409286144 | bytes 6619136 | tf_op jit(solution)/shard_map/dot_general | solution.py:65
  216.0 0.0 slice-start
  216.0 0.0 slice-start.1
  216.0 5.7 %fusion.3 = f32[1024,896]{1,0:T(8,128)} fusion(bf16[6144,1024]{1,0:T(8,128)(2,1)} %copy-done, bf16[6144,896]{1,0:T(8,128)(2,1)} %all-gather.4.cloned.1.call-done), kind=kOutput, calls=%fused_computation.5 | convolution fusion | flops 1409286144 | bytes 6619136 | tf_op jit(solution)/shard_map/dot_general | solution.py:65
  221.7 0.0 copy-done.1
  221.7 0.0 slice-start.2
  221.7 5.1 %fusion.5 = f32[1024,896]{1,0:T(8,128)} fusion(bf16[6144,1024]{1,0:T(8,128)(2,1)S(1)} %copy-done.1, bf16[6144,896]{1,0:T(8,128)(2,1)} %all-gather.4.cloned.1.call-done), kind=kOutput, calls=%fused_computation.7 | convolution fusion | flops 1409286144 | bytes 6619136 | tf_op jit(solution)/shard_map/dot_general | solution.py:65
  226.9 0.0 slice-done
  226.9 0.0 slice-done.1
  226.9 0.0 slice-done.2
  226.9 3.7 fusion.7
  230.6 3.7 fusion.9
  234.3 3.6 fusion.11
  237.9 3.7 fusion.13
  241.6 104.1 %all-reduce.2.cloned.1.call-done = bf16[768,768]{1,0:T(8,128)(2,1)} async-done(((bf16[768,768]{1,0:T(8,128)(2,1)}), bf16[768,768]{1,0:T(8,128)(2,1)}) %all-reduce.2.cloned.1.call-update) | async-done | bytes 1179664 | tf_op jit(solution)/shard_map/psum | solution.py:43
  345.7 35.8 %reduce-scatter.2.cloned.1.call-done = bf16[24,768]{1,0:T(8,128)(2,1)} async-done(((bf16[192,768]{1,0:T(8,128)(2,1)}), bf16[24,768]{1,0:T(8,128)(2,1)}) %reduce-scatter.2.cloned.1.call-update) | async-done | bytes 36880 | tf_op jit(solution)/shard_map/reduce_scatter | solution.py:52
  381.5 1.4 multiply_reduce_fusion
  382.9 0.6 fusion.39
  383.5 59.2 %all-gather = f32[256,1,8]{2,1,0:T(1,128)S(1)} all-gather(f32[1,1,8]{2,1,0:T(1,128)S(1)} %fusion.39), channel_id=1, replica_groups=mesh['row'=32,'col'=8] {'row','col'}, dimensions={0}, use_global_device_ids=true | all-gather | bytes 8224 | tf_op jit(solution)/shard_map/all_gather | solution.py:9
  442.8 0.3 reduce_sum.29
  443.0 0.5 add_divide_fusion
  443.6 0.7 fusion.40
  444.2 17.6 %fusion.17 = bf16[896,1024]{0,1:T(8,128)(2,1)S(1)} fusion(bf16[6144,1024]{1,0:T(8,128)(2,1)} %copy-done, f32[]{:T(128)} %bitcast.12, f32[1024,896]{1,0:T(8,128)} %fusion.1, f32[]{:T(128)} %bitcast.11, f32[1024,896]{1,0:T(8,128)} %fusion.3, f32[]{:T(128)} %bitcast.10, f32[1024,896]{1,0:T(8,128)} %fusion.5, f32[]{:T(128)} %bitcast.9, f32[1024,896]{1,0:T(8,128)} %fusion.7, ...), kind=kOutput, calls=%fused_computation.19 | convolution fusion | flops 1424883712 | bytes 30478336 | tf_op jit(solution)/shard_map/dot_general | solution.py:65
  461.9 2.4 copy.10
  (3 shorter events, 0.0 us)
Async XLA Ops:
  7.2 70.1 %all-gather.4.cloned.1.call-start = ((), (), s32[]{:S(2)}) async-start(), calls=%async_computation.1 | async-start | bytes 12386304 | tf_op jit(solution)/shard_map/all_gather | solution.py:33
  7.9 190.0 %all-gather.6.cloned.1.call-start = ((), (), s32[]{:S(2)}) async-start(), calls=%async_computation.3 | async-start | bytes 12976128 | tf_op jit(solution)/shard_map/all_gather | solution.py:34
  8.6 337.1 %all-reduce.2.cloned.1.call-start = ((), (), s32[]{:S(2)}) async-start(), calls=%async_computation.2 | async-start | bytes 2359296 | tf_op jit(solution)/shard_map/psum | solution.py:43
  87.4 294.1 %reduce-scatter.2.cloned.1.call-start = ((), (), s32[]{:S(2)}) async-start(), calls=%async_computation.4 | async-start | bytes 331776 | tf_op jit(solution)/shard_map/reduce_scatter | solution.py:52
  204.3 4.5 copy-start
  210.3 11.4 %copy-start.1 = (bf16[6144,1024]{1,0:T(8,128)(2,1)S(1)}, bf16[6144,1024]{1,0:T(8,128)(2,1)}, u32[]{:S(2)}) copy-start(bf16[6144,1024]{1,0:T(8,128)(2,1)} %copy-done) | copy-start | bytes 37748740
  216.0 10.9 %slice-start = ((s8[11010048]{0:T(1024)(128)(4,1)}), s8[4194304]{0:T(1024)(128)(4,1)S(1)}, s32[]{:S(2)}) async-start(s8[11010048]{0:T(1024)(128)(4,1)} %bitcast.22), calls=%async_computation.5 | async-start | bytes 8388608
  216.0 10.9 %slice-start.1 = ((s8[11010048]{0:T(1024)(128)(4,1)}), s8[4194304]{0:T(1024)(128)(4,1)S(1)}, s32[]{:S(2)}) async-start(s8[11010048]{0:T(1024)(128)(4,1)} %bitcast.22), calls=%async_computation.6 | async-start | bytes 8388608
  221.7 5.2 %slice-start.2 = ((s8[11010048]{0:T(1024)(128)(4,1)}), s8[2621440]{0:T(1024)(128)(4,1)S(1)}, s32[]{:S(2)}) async-start(s8[11010048]{0:T(1024)(128)(4,1)} %bitcast.22), calls=%async_computation.7 | async-start | bytes 5242880
Sparse Core Ops, SparseCore 0:
  9.8 67.3 all-gather.3
  79.8 118.0 all-gather.5
  201.9 143.7 all-reduce.1
  348.1 33.3 reduce-scatter.1
